TPU v7x, 32 devices: a whole 2x2x4 slice. The times are simulated.
32 devices in a mesh: sec: 4 (over y, x), tile: 8 (over z, core).
Axes of the slice: x: 2, y: 2, z: 4, core: 2. Of those that a mesh axis runs over, the one named last changes fastest.
Arguments:
- pan_source: bfloat16 [32, 256, 384], P(('sec', 'tile'))
- ms_source: bfloat16 [8, 32, 64, 96], P(None, ('sec', 'tile'))
- row_tap: int32 [32, 256], P(('sec', 'tile')), may hold values from 0 to 316, as said below
- row_frac: float32 [32, 256], P(('sec', 'tile')), may hold values from 0 to 1
- col_tap: int32 [32, 384], P(('sec', 'tile')), may hold values from 0 to 444, as said below
- col_frac: float32 [32, 384], P(('sec', 'tile')), may hold values from 0 to 1
- ms_row_tap: int32 [32, 256], P(('sec', 'tile')), may hold values from 0 to 76, as said below
- ms_row_frac: float32 [32, 256], P(('sec', 'tile')), may hold values from 0 to 1
- ms_col_tap: int32 [32, 384], P(('sec', 'tile')), may hold values from 0 to 108, as said below
- ms_col_frac: float32 [32, 384], P(('sec', 'tile')), may hold values from 0 to 1
Outputs:
- ms_sharp: bfloat16 [8, 32, 256, 384], P(None, ('sec', 'tile'))
Inputs may be any that keep to these rules, and one draw needn't show every extreme that they name: Each row of row_tap starts at 0 and rises by 0, 1 or 2 from one map row to the next. Each row of col_tap starts at 0 and rises by 0, 1 or 2 from one map column to the next. Each row of ms_row_tap starts at 0 and rises by 0 or 1 from one map row to the next. Each row of ms_col_tap starts at 0 and rises by 0 or 1 from one map column to the next.
All inputs are finite; a program needn't handle non-finite values.
Results may differ from a plain program's by a relative error of at most 0.0045.
Values may be sent and summed in bfloat16 or wider, within the bound.
A program may use at most 128 MiB of HBM per device.

v0:
```python
import jax
import jax.numpy as jnp
from jax import lax
from jax.sharding import PartitionSpec as P

HALO = 32
MHALO = 8
RADIUS = 8


EPSILON = 0.1


def passed_along(value, axis, steps):
    count = lax.axis_size(axis)
    pairs = [(source, (source + steps) % count) for source in range(count)]
    return lax.ppermute(value, axis, pairs)


def cubic_weights(fraction):
    squared = fraction * fraction
    cubed = squared * fraction
    return jnp.stack(
        [
            -0.5 * cubed + squared - 0.5 * fraction,
            1.5 * cubed - 2.5 * squared + 1.0,
            -1.5 * cubed + 2.0 * squared + 0.5 * fraction,
            0.5 * cubed - 0.5 * squared,
        ],
        axis=0,
    )


def band_matrix(first_taps, fraction, length):
    weights = cubic_weights(fraction)
    position = lax.broadcasted_iota(jnp.int32, (first_taps.shape[0], length), 1)
    matrix = jnp.zeros((first_taps.shape[0], length), jnp.float32)
    for offset in range(4):
        matrix = matrix + jnp.where(
            position == first_taps[:, None] + offset, weights[offset][:, None], 0.0
        )
    return matrix.astype(jnp.bfloat16)


def window_sum(values, along_axis, window):
    total_length = values.shape[along_axis]
    kept_length = total_length - window + 1
    result = None
    partial_value = values
    stride = 1
    begin_at = 0
    while stride <= window:
        if window & stride:
            addend = lax.slice_in_dim(
                partial_value, begin_at, begin_at + kept_length, axis=along_axis
            )
            result = addend if result is None else result + addend
            begin_at = begin_at + stride
        if stride * 2 <= window:
            extent = partial_value.shape[along_axis]
            partial_value = lax.slice_in_dim(
                partial_value, 0, extent - stride, axis=along_axis
            ) + lax.slice_in_dim(partial_value, stride, extent, axis=along_axis)
        stride = stride * 2
    return result


def box_sum(values, radius):
    window = 2 * radius + 1
    return window_sum(window_sum(values, 1, window), 2, window)


def coverage(anchor, amount, extent, radius):
    places = anchor + lax.iota(jnp.int32, amount)
    highest = jnp.minimum(places + radius, extent - 1)
    lowest = jnp.maximum(places - radius, 0)
    return (highest - lowest + 1).astype(jnp.float32)


def widen_tile(tile_block, strip_depth, column, grid_row, grid_total):
    rows_now = tile_block.shape[1]
    cols_now = tile_block.shape[2]
    west_ok = (column > 0).astype(tile_block.dtype)
    east_ok = (column < 3).astype(tile_block.dtype)
    north_ok = (grid_row > 0).astype(tile_block.dtype)
    south_ok = (grid_row < grid_total - 1).astype(tile_block.dtype)
    above_below = []
    for distance in (4, -4):
        outgoing = (
            tile_block[:, rows_now - strip_depth :, :]
            if distance > 0
            else tile_block[:, :strip_depth, :]
        )
        above_below.append(passed_along(outgoing, ("sec", "tile"), distance))
    heightened = jnp.concatenate(
        [above_below[0] * north_ok, tile_block, above_below[1] * south_ok], axis=1
    )
    side_parts = []
    for distance in (1, -1):
        outgoing = (
            heightened[:, :, cols_now - strip_depth :]
            if distance > 0
            else heightened[:, :, :strip_depth]
        )
        side_parts.append(passed_along(outgoing, ("sec", "tile"), distance))
    return jnp.concatenate([side_parts[0] * west_ok, heightened, side_parts[1] * east_ok], axis=2)


def resample_tile(extended, first_rows, row_fracs, first_cols, col_fracs):
    row_matrix = band_matrix(first_rows, row_fracs, extended.shape[1])
    col_matrix = band_matrix(first_cols, col_fracs, extended.shape[2])
    row_segment = jnp.einsum(
        "ij,cjk->cik", row_matrix, extended, preferred_element_type=jnp.float32
    ).astype(jnp.bfloat16)
    return jnp.einsum(
        "cik,lk->cil", row_segment, col_matrix, preferred_element_type=jnp.float32
    ).astype(jnp.bfloat16)


def fit_gain(widened, coverage_map):
    guide_wide = widened[0].astype(jnp.float32)
    bands_wide = widened[1:].astype(jnp.float32)
    band_count = bands_wide.shape[0]
    stacked = jnp.concatenate(
        [
            guide_wide[None],
            (guide_wide * guide_wide)[None],
            bands_wide,
            guide_wide[None] * bands_wide,
        ],
        axis=0,
    )
    box_means = box_sum(stacked, RADIUS) / coverage_map[None]
    mean_guide = box_means[0]
    mean_square = box_means[1]
    mean_bands = box_means[2 : 2 + band_count]
    mean_cross = box_means[2 + band_count :]
    variance = mean_square - mean_guide * mean_guide
    gain_map = (mean_cross - mean_guide[None] * mean_bands) / (variance[None] + EPSILON)
    offset_map = mean_bands - gain_map * mean_guide[None]
    return (gain_map, offset_map)


def local(
    pan_source,
    ms_source,
    row_tap,
    row_frac,
    col_tap,
    col_frac,
    ms_row_tap,
    ms_row_frac,
    ms_col_tap,
    ms_col_frac,
):
    tile_rows = pan_source.shape[1]
    tile_cols = pan_source.shape[2]
    total_tiles = lax.axis_size(("sec", "tile"))
    placed = (lax.axis_index(("sec", "tile")) + 2) % total_tiles
    column = placed % 4
    grid_row = placed // 4
    grid_total = total_tiles // 4
    map_rows = grid_total * tile_rows
    map_cols = 4 * tile_cols
    pan_wide = widen_tile(pan_source, HALO, column, grid_row, grid_total)
    ms_wide = widen_tile(ms_source[:, 0], MHALO, column, grid_row, grid_total)
    pan_image = resample_tile(pan_wide, row_tap[0], row_frac[0], col_tap[0], col_frac[0])
    ms_image = resample_tile(ms_wide, ms_row_tap[0], ms_row_frac[0], ms_col_tap[0], ms_col_frac[0])
    resampled = jnp.concatenate([pan_image, ms_image], axis=0)
    guide_image = resampled[0].astype(jnp.float32)
    row_cover = coverage(grid_row * tile_rows, tile_rows, map_rows, RADIUS)
    col_cover = coverage(column * tile_cols, tile_cols, map_cols, RADIUS)
    coverage_map = row_cover[:, None] * col_cover[None, :]
    widened = widen_tile(resampled, 2 * RADIUS, column, grid_row, grid_total)
    row_anchor = grid_row * tile_rows - RADIUS
    col_anchor = column * tile_cols - RADIUS
    row_wide = coverage(row_anchor, tile_rows + 2 * RADIUS, map_rows, RADIUS)
    col_wide = coverage(col_anchor, tile_cols + 2 * RADIUS, map_cols, RADIUS)
    gain_map, offset_map = fit_gain(widened, row_wide[:, None] * col_wide[None, :])
    row_places = row_anchor + lax.iota(jnp.int32, tile_rows + 2 * RADIUS)
    col_places = col_anchor + lax.iota(jnp.int32, tile_cols + 2 * RADIUS)
    row_inside = (row_places >= 0) & (row_places < map_rows)
    col_inside = (col_places >= 0) & (col_places < map_cols)
    inside_mask = (row_inside[:, None] & col_inside[None, :]).astype(jnp.bfloat16)
    fitted = (
        jnp.concatenate([gain_map, offset_map], axis=0).astype(jnp.bfloat16) * inside_mask[None]
    )
    fitted_wide = lax.optimization_barrier(fitted).astype(jnp.float32)
    smooth = box_sum(fitted_wide, RADIUS) / coverage_map[None]
    band_count = smooth.shape[0] // 2
    sharpened = (smooth[:band_count] * guide_image[None] + smooth[band_count:]).astype(jnp.bfloat16)
    return sharpened[:, None]


def solution(mesh):
    placed = (
        P(("sec", "tile"), None, None),
        P(None, ("sec", "tile"), None, None),
        P(("sec", "tile"), None),
        P(("sec", "tile"), None),
        P(("sec", "tile"), None),
        P(("sec", "tile"), None),
        P(("sec", "tile"), None),
        P(("sec", "tile"), None),
        P(("sec", "tile"), None),
        P(("sec", "tile"), None),
    )
    return jax.shard_map(
        local,
        mesh=mesh,
        in_specs=placed,
        out_specs=P(None, ("sec", "tile"), None, None),
        check_vma=False,
    )
```

profile of v0, /device:TPU:0, one launch (start us, length us, event | category | flops | bytes accessed | tf_op | source)
XLA Modules:
  0.0 291.6 jit_solution(5972369763596056490)
XLA Ops:
  0.0 0.8 fusion.139
  0.8 5.9 %collective-permute-start.1 = (bf16[1,32,384]{2,1,0:T(8,128)(2,1)S(1)}, bf16[1,32,384]{2,1,0:T(8,128)(2,1)S(1)}, u32[]{:S(2)}, u32[]{:S(2)}) collective-permute-start(bf16[1,32,384]{2,1,0:T(8,128)(2,1)S(1)} %get-tuple-element.26), channel_id=1, source_target_pairs={{0,28},{1,29},{2,30},{3,31},{4,0},{5,1},{6,2},{7,3},{8,4},{9,5},{1... | collective-permute-start | bytes 73736 | tf_op jit(solution)/shard_map/ppermute | solution.py:17
  6.7 0.7 fusion.141
  7.4 2.0 collective-permute-start.4
  9.4 2.8 collective-permute-start.5
  12.2 0.7 reduce.1
  12.9 0.7 reduce
  13.6 0.7 add_subtract_fusion.1
  14.3 0.7 broadcast_add_fusion.11
  15.0 0.7 reduce.3
  15.7 0.7 reduce.2
  16.4 0.7 add_subtract_fusion
  17.1 0.9 broadcast_multiply_fusion.1
  18.0 0.8 broadcast_multiply_fusion.2
  18.8 0.7 broadcast_add_fusion.10
  19.6 0.9 pad_maximum_fusion.10
  20.5 0.1 fusion.140
  20.7 5.3 %collective-permute-start.7 = (bf16[8,80,8]{2,1,0:T(8,128)(2,1)S(1)}, bf16[8,80,8]{2,1,0:T(8,128)(2,1)S(1)}, u32[]{:S(2)}, u32[]{:S(2)}) collective-permute-start(bf16[8,80,8]{2,1,0:T(8,128)(2,1)S(1)} %get-tuple-element.28), channel_id=1, source_target_pairs={{0,31},{1,0},{2,1},{3,2},{4,3},{5,4},{6,5},{7,6},{8,7},{9,8},{10,9... | collective-permute-start | bytes 30728 | tf_op jit(solution)/shard_map/ppermute | solution.py:17
  26.0 4.2 %collective-permute-done.6 = bf16[8,80,8]{2,1,0:T(8,128)(2,1)S(1)} collective-permute-done((bf16[8,80,8]{2,1,0:T(8,128)(2,1)S(1)}, bf16[8,80,8]{2,1,0:T(8,128)(2,1)S(1)}, u32[]{:S(2)}, u32[]{:S(2)}) %collective-permute-start.6) | collective-permute-done | bytes 10272 | tf_op jit(solution)/shard_map/ppermute | solution.py:17
  30.3 1.0 pad_maximum_fusion.15
  31.3 2.0 convolution_convert_fusion
  33.4 5.4 %collective-permute-start.3 = (bf16[1,320,32]{2,1,0:T(8,128)(2,1)S(1)}, bf16[1,320,32]{2,1,0:T(8,128)(2,1)S(1)}, u32[]{:S(2)}, u32[]{:S(2)}) collective-permute-start(bf16[1,320,32]{2,1,0:T(8,128)(2,1)S(1)} %get-tuple-element.24), channel_id=1, source_target_pairs={{0,31},{1,0},{2,1},{3,2},{4,3},{5,4},{6,5},{7,6},{8,7},{9,8},{10,9... | collective-permute-start | bytes 61448 | tf_op jit(solution)/shard_map/ppermute | solution.py:17
  38.8 2.0 collective-permute-done.3
  40.8 3.4 %fusion.142 = (f32[256,384]{1,0:T(8,128)}, bf16[256,384]{1,0:T(8,128)(2,1)S(1)}) fusion(f32[384]{0:T(512)S(1)} %get-tuple-element.32, s32[384]{0:T(512)S(1)} %get-tuple-element.36, f32[384]{0:T(512)S(1)} %get-tuple-element.34, s32[384]{0:T(512)S(1)} %get-tuple-element.37, f32[384]{0:T(512)S(1)} %get-tuple-element.33, s32[384]{0:T(512)S(1)} %get-tuple-element.35, ...), kind=kOutput, calls=%fused_computation.219 | convolution fusion | flops 166273024 | bytes 897024 | tf_op jit(solution)/shard_map/cik,lk->cil/dot_general | solution.py:115
  44.3 4.7 %collective-permute-start.9 = (bf16[9,16,384]{2,1,0:T(8,128)(2,1)S(1)}, bf16[9,16,384]{2,1,0:T(8,128)(2,1)S(1)}, u32[]{:S(2)}, u32[]{:S(2)}) collective-permute-start(bf16[9,16,384]{2,1,0:T(8,128)(2,1)S(1)} %get-tuple-element.22), channel_id=1, source_target_pairs={{0,28},{1,29},{2,30},{3,31},{4,0},{5,1},{6,2},{7,3},{8,4},{9,5},{1... | collective-permute-start | bytes 331784 | tf_op jit(solution)/shard_map/ppermute | solution.py:17
  49.0 3.9 %collective-permute-done.8 = bf16[9,16,384]{2,1,0:T(8,128)(2,1)S(1)} collective-permute-done((bf16[9,16,384]{2,1,0:T(8,128)(2,1)S(1)}, bf16[9,16,384]{2,1,0:T(8,128)(2,1)S(1)}, u32[]{:S(2)}, u32[]{:S(2)}) %collective-permute-start.8) | collective-permute-done | bytes 110624 | tf_op jit(solution)/shard_map/ppermute | solution.py:17
  52.9 0.3 pad_maximum_fusion.9
  53.2 0.3 copy.19
  53.6 0.8 and_convert_fusion
  54.4 0.3 copy.20
  54.7 5.6 %collective-permute-start.11 = (bf16[9,288,16]{1,2,0:T(8,128)(2,1)S(1)}, bf16[9,288,16]{1,2,0:T(8,128)(2,1)S(1)}, u32[]{:S(2)}, u32[]{:S(2)}) collective-permute-start(bf16[9,288,16]{1,2,0:T(8,128)(2,1)S(1)} %copy.20), channel_id=1, source_target_pairs={{0,31},{1,0},{2,1},{3,2},{4,3},{5,4},{6,5},{7,6},{8,7},{9,8},{10,9... | collective-permute-start | bytes 248840 | tf_op jit(solution)/shard_map/ppermute | solution.py:17
  60.3 1.1 collective-permute-done.10
  61.4 0.4 copy.21
  61.7 0.9 collective-permute-done.11
  62.6 0.3 copy.22
  63.0 2.3 fusion.8
  65.2 0.2 fusion.134
  65.5 2.6 broadcast_multiply_fusion
  68.0 1.2 pad_maximum_fusion
  69.2 4.6 %slice_add_fusion.2 = f32[18,287,416]{2,1,0:T(8,128)} fusion(f32[18,288,416]{2,1,0:T(8,128)S(1)} %pad_maximum_fusion), kind=kLoop, calls=%fused_computation.2 | loop fusion | flops 2149056 | bytes 25788672 | tf_op jit(solution)/shard_map/add | solution.py:61
  73.9 9.7 %slice_add_fusion.1 = f32[18,285,416]{2,1,0:T(8,128)S(1)} fusion(f32[18,287,416]{2,1,0:T(8,128)} %slice_add_fusion.2), kind=kLoop, calls=%fused_computation.1 | loop fusion | flops 2134080 | bytes 25608960 | tf_op jit(solution)/shard_map/add | solution.py:61
  83.6 4.6 %slice_add_fusion = f32[18,281,416]{2,1,0:T(8,128)} fusion(f32[18,285,416]{2,1,0:T(8,128)S(1)} %slice_add_fusion.1), kind=kLoop, calls=%fused_computation | loop fusion | flops 2104128 | bytes 25249536 | tf_op jit(solution)/shard_map/add | solution.py:61
  88.2 12.1 %fusion.135 = (f32[18,273,416]{2,1,0:T(8,128)S(1)}, f32[18,273,416]{2,1,0:T(8,128)}) fusion(f32[18,281,416]{2,1,0:T(8,128)} %slice_add_fusion), kind=kLoop, calls=%fused_computation.212 | loop fusion | bytes 32707584 | tf_op jit(solution)/shard_map/slice | solution.py:61
  100.3 11.1 %fusion.2 = f32[18,272,416]{2,1,0:T(8,128)} fusion(f32[18,273,416]{2,1,0:T(8,128)} %get-tuple-element.10, f32[18,273,416]{2,1,0:T(8,128)S(1)} %get-tuple-element.9, f32[18,288,416]{2,1,0:T(8,128)S(1)} %pad_maximum_fusion), kind=kLoop, calls=%fused_computation.11 | loop fusion | flops 4073472 | bytes 32587776 | tf_op jit(solution)/shard_map/add | solution.py:57
  111.4 13.3 %slice_add_fusion.6 = f32[18,272,415]{2,1,0:T(8,128)} fusion(f32[18,272,416]{2,1,0:T(8,128)} %fusion.2), kind=kLoop, calls=%fused_computation.9 | loop fusion | flops 2031840 | bytes 24382080 | tf_op jit(solution)/shard_map/add | solution.py:61
  124.7 13.1 %slice_add_fusion.5 = f32[18,272,413]{2,1,0:T(8,128)} fusion(f32[18,272,415]{2,1,0:T(8,128)} %slice_add_fusion.6), kind=kLoop, calls=%fused_computation.8 | loop fusion | flops 2022048 | bytes 24264576 | tf_op jit(solution)/shard_map/add | solution.py:61
  137.8 13.3 %slice_add_fusion.4 = f32[18,272,409]{2,1,0:T(8,128)} fusion(f32[18,272,413]{2,1,0:T(8,128)} %slice_add_fusion.5), kind=kLoop, calls=%fused_computation.7 | loop fusion | flops 2002464 | bytes 24029568 | tf_op jit(solution)/shard_map/add | solution.py:61
  151.0 14.3 %fusion.136 = (f32[18,272,401]{2,1,0:T(8,128)S(1)}, f32[18,272,401]{2,1,0:T(8,128)}) fusion(f32[18,272,409]{2,1,0:T(8,128)} %slice_add_fusion.4), kind=kLoop, calls=%fused_computation.213 | loop fusion | bytes 31412736 | tf_op jit(solution)/shard_map/slice | solution.py:61
  165.4 9.9 %fusion.1 = f32[18,272,400]{2,1,0:T(8,128)S(1)} fusion(f32[18,272,401]{2,1,0:T(8,128)} %get-tuple-element.14, f32[18,272,401]{2,1,0:T(8,128)S(1)} %get-tuple-element.13, f32[18,272,416]{2,1,0:T(8,128)} %fusion.2, f32[272,400]{1,0:T(8,128)S(1)} %copy-done), kind=kLoop, calls=%fused_computation.6 | loop fusion | flops 5875200 | bytes 31769600 | tf_op jit(solution)/shard_map/div | solution.py:133
  175.2 0.1 fusion.13
  175.4 1.9 fusion.133
  177.3 0.6 maximum_multiply_fusion
  177.9 4.7 %convert_element_type.132 = f32[16,272,400]{2,1,0:T(8,128)} convert(bf16[16,272,400]{2,1,0:T(8,128)(2,1)S(1)} %maximum_multiply_fusion) | non-fusion elementwise | flops 1740800 | bytes 10444800 | tf_op jit(solution)/shard_map/convert_element_type | solution.py:188
  182.6 12.1 %slice_add_fusion.10 = f32[16,271,400]{2,1,0:T(8,128)} fusion(f32[16,272,400]{2,1,0:T(8,128)} %convert_element_type.132), kind=kLoop, calls=%fused_computation.14 | loop fusion | flops 1734400 | bytes 20812800 | tf_op jit(solution)/shard_map/add | solution.py:61
  194.8 12.3 %slice_add_fusion.9 = f32[16,269,400]{2,1,0:T(8,128)} fusion(f32[16,271,400]{2,1,0:T(8,128)} %slice_add_fusion.10), kind=kLoop, calls=%fused_computation.13 | loop fusion | flops 1721600 | bytes 20659200 | tf_op jit(solution)/shard_map/add | solution.py:61
  207.1 12.2 %slice_add_fusion.8 = f32[16,265,400]{2,1,0:T(8,128)} fusion(f32[16,269,400]{2,1,0:T(8,128)} %slice_add_fusion.9), kind=kLoop, calls=%fused_computation.12 | loop fusion | flops 1696000 | bytes 20352000 | tf_op jit(solution)/shard_map/add | solution.py:61
  219.3 7.2 %fusion.137 = (f32[16,257,400]{2,1,0:T(8,128)S(1)}, f32[16,257,400]{2,1,0:T(8,128)S(1)}) fusion(f32[16,265,400]{2,1,0:T(8,128)} %slice_add_fusion.8), kind=kLoop, calls=%fused_computation.214 | loop fusion | bytes 26316800 | tf_op jit(solution)/shard_map/slice | solution.py:61
  226.6 7.6 %fusion.3 = f32[16,256,400]{2,1,0:T(8,128)} fusion(f32[16,257,400]{2,1,0:T(8,128)S(1)} %get-tuple-element.16, f32[16,257,400]{2,1,0:T(8,128)S(1)} %get-tuple-element.15, f32[16,272,400]{2,1,0:T(8,128)} %convert_element_type.132), kind=kLoop, calls=%fused_computation.19 | loop fusion | flops 3276800 | bytes 26214400 | tf_op jit(solution)/shard_map/add | solution.py:57
  234.2 11.4 %slice_add_fusion.13 = f32[16,256,399]{2,1,0:T(8,128)} fusion(f32[16,256,400]{2,1,0:T(8,128)} %fusion.3), kind=kLoop, calls=%fused_computation.17 | loop fusion | flops 1634304 | bytes 19611648 | tf_op jit(solution)/shard_map/add | solution.py:61
  245.6 11.5 %slice_add_fusion.12 = f32[16,256,397]{2,1,0:T(8,128)} fusion(f32[16,256,399]{2,1,0:T(8,128)} %slice_add_fusion.13), kind=kLoop, calls=%fused_computation.16 | loop fusion | flops 1626112 | bytes 19513344 | tf_op jit(solution)/shard_map/add | solution.py:61
  257.2 11.5 %slice_add_fusion.11 = f32[16,256,393]{2,1,0:T(8,128)} fusion(f32[16,256,397]{2,1,0:T(8,128)} %slice_add_fusion.12), kind=kLoop, calls=%fused_computation.15 | loop fusion | flops 1609728 | bytes 19316736 | tf_op jit(solution)/shard_map/add | solution.py:61
  268.7 10.9 %fusion.138 = (f32[16,256,385]{2,1,0:T(8,128)S(1)}, f32[16,256,385]{2,1,0:T(8,128)}) fusion(f32[16,256,393]{2,1,0:T(8,128)} %slice_add_fusion.11), kind=kLoop, calls=%fused_computation.215 | loop fusion | bytes 25231360 | tf_op jit(solution)/shard_map/slice | solution.py:61
  279.6 7.4 %fusion.5 = f32[16,256,384]{2,1,0:T(8,128)} fusion(f32[16,256,385]{2,1,0:T(8,128)} %get-tuple-element.18, f32[16,256,385]{2,1,0:T(8,128)S(1)} %get-tuple-element.17, f32[16,256,400]{2,1,0:T(8,128)S(1)} %bitcast.43, f32[256,384]{1,0:T(8,128)S(1)} %copy-done.1), kind=kLoop, calls=%fused_computation.22 | loop fusion | flops 4718592 | bytes 25559040 | tf_op jit(solution)/shard_map/div | solution.py:189
  287.0 4.4 %fusion.9 = bf16[8,1,256,384]{3,2,1,0:T(8,128)(2,1)} fusion(f32[16,256,384]{2,1,0:T(8,128)} %fusion.5, f32[256,384]{1,0:T(8,128)S(1)} %copy-done.3), kind=kLoop, calls=%fused_computation.38 | loop fusion | flops 2359296 | bytes 8257536 | tf_op jit(solution)/shard_map/broadcast_in_dim | solution.py:192
  (48 shorter events, 0.6 us)
Async XLA Ops:
  0.8 29.5 %collective-permute-start.1 = (bf16[1,32,384]{2,1,0:T(8,128)(2,1)S(1)}, bf16[1,32,384]{2,1,0:T(8,128)(2,1)S(1)}, u32[]{:S(2)}, u32[]{:S(2)}) collective-permute-start(bf16[1,32,384]{2,1,0:T(8,128)(2,1)S(1)} %get-tuple-element.26), channel_id=1, source_target_pairs={{0,28},{1,29},{2,30},{3,31},{4,0},{5,1},{6,2},{7,3},{8,4},{9,5},{1... | collective-permute-start | bytes 73736 | tf_op jit(solution)/shard_map/ppermute | solution.py:17
  6.7 23.6 %collective-permute-start = (bf16[1,32,384]{2,1,0:T(8,128)(2,1)S(1)}, bf16[1,32,384]{2,1,0:T(8,128)(2,1)S(1)}, u32[]{:S(2)}, u32[]{:S(2)}) collective-permute-start(bf16[1,32,384]{2,1,0:T(8,128)(2,1)S(1)} %get-tuple-element.25), channel_id=1, source_target_pairs={{0,4},{1,5},{2,6},{3,7},{4,8},{5,9},{6,10},{7,11},{8,12},{9,13},{1... | collective-permute-start | bytes 73736 | tf_op jit(solution)/shard_map/ppermute | solution.py:17
  7.4 12.1 %collective-permute-start.4 = (bf16[8,8,96]{2,1,0:T(8,128)(2,1)S(1)}, bf16[8,8,96]{2,1,0:T(8,128)(2,1)S(1)}, u32[]{:S(2)}, u32[]{:S(2)}) collective-permute-start(bf16[8,8,96]{2,1,0:T(8,128)(2,1)S(1)} %get-tuple-element.29), channel_id=1, source_target_pairs={{0,4},{1,5},{2,6},{3,7},{4,8},{5,9},{6,10},{7,11},{8,12},{9,13},{1... | collective-permute-start | bytes 36872 | tf_op jit(solution)/shard_map/ppermute | solution.py:17
  9.4 10.2 %collective-permute-start.5 = (bf16[8,8,96]{2,1,0:T(8,128)(2,1)S(1)}, bf16[8,8,96]{2,1,0:T(8,128)(2,1)S(1)}, u32[]{:S(2)}, u32[]{:S(2)}) collective-permute-start(bf16[8,8,96]{2,1,0:T(8,128)(2,1)S(1)} %get-tuple-element.30), channel_id=1, source_target_pairs={{0,28},{1,29},{2,30},{3,31},{4,0},{5,1},{6,2},{7,3},{8,4},{9,5},{1... | collective-permute-start | bytes 36872 | tf_op jit(solution)/shard_map/ppermute | solution.py:17
  20.6 9.6 %collective-permute-start.6 = (bf16[8,80,8]{2,1,0:T(8,128)(2,1)S(1)}, bf16[8,80,8]{2,1,0:T(8,128)(2,1)S(1)}, u32[]{:S(2)}, u32[]{:S(2)}) collective-permute-start(bf16[8,80,8]{2,1,0:T(8,128)(2,1)S(1)} %get-tuple-element.27), channel_id=1, source_target_pairs={{0,1},{1,2},{2,3},{3,4},{4,5},{5,6},{6,7},{7,8},{8,9},{9,10},{10,1... | collective-permute-start | bytes 30728 | tf_op jit(solution)/shard_map/ppermute | solution.py:17
  20.7 9.5 %collective-permute-start.7 = (bf16[8,80,8]{2,1,0:T(8,128)(2,1)S(1)}, bf16[8,80,8]{2,1,0:T(8,128)(2,1)S(1)}, u32[]{:S(2)}, u32[]{:S(2)}) collective-permute-start(bf16[8,80,8]{2,1,0:T(8,128)(2,1)S(1)} %get-tuple-element.28), channel_id=1, source_target_pairs={{0,31},{1,0},{2,1},{3,2},{4,3},{5,4},{6,5},{7,6},{8,7},{9,8},{10,9... | collective-permute-start | bytes 30728 | tf_op jit(solution)/shard_map/ppermute | solution.py:17
  31.3 7.5 %collective-permute-start.2 = (bf16[1,320,32]{2,1,0:T(8,128)(2,1)S(1)}, bf16[1,320,32]{2,1,0:T(8,128)(2,1)S(1)}, u32[]{:S(2)}, u32[]{:S(2)}) collective-permute-start(bf16[1,320,32]{2,1,0:T(8,128)(2,1)S(1)} %get-tuple-element.23), channel_id=1, source_target_pairs={{0,1},{1,2},{2,3},{3,4},{4,5},{5,6},{6,7},{7,8},{8,9},{9,10},{10,1... | collective-permute-start | bytes 61448 | tf_op jit(solution)/shard_map/ppermute | solution.py:17
  33.4 7.4 %collective-permute-start.3 = (bf16[1,320,32]{2,1,0:T(8,128)(2,1)S(1)}, bf16[1,320,32]{2,1,0:T(8,128)(2,1)S(1)}, u32[]{:S(2)}, u32[]{:S(2)}) collective-permute-start(bf16[1,320,32]{2,1,0:T(8,128)(2,1)S(1)} %get-tuple-element.24), channel_id=1, source_target_pairs={{0,31},{1,0},{2,1},{3,2},{4,3},{5,4},{6,5},{7,6},{8,7},{9,8},{10,9... | collective-permute-start | bytes 61448 | tf_op jit(solution)/shard_map/ppermute | solution.py:17
  44.2 8.7 %collective-permute-start.8 = (bf16[9,16,384]{2,1,0:T(8,128)(2,1)S(1)}, bf16[9,16,384]{2,1,0:T(8,128)(2,1)S(1)}, u32[]{:S(2)}, u32[]{:S(2)}) collective-permute-start(bf16[9,16,384]{2,1,0:T(8,128)(2,1)S(1)} %get-tuple-element.21), channel_id=1, source_target_pairs={{0,4},{1,5},{2,6},{3,7},{4,8},{5,9},{6,10},{7,11},{8,12},{9,13},{1... | collective-permute-start | bytes 331784 | tf_op jit(solution)/shard_map/ppermute | solution.py:17
  44.3 8.6 %collective-permute-start.9 = (bf16[9,16,384]{2,1,0:T(8,128)(2,1)S(1)}, bf16[9,16,384]{2,1,0:T(8,128)(2,1)S(1)}, u32[]{:S(2)}, u32[]{:S(2)}) collective-permute-start(bf16[9,16,384]{2,1,0:T(8,128)(2,1)S(1)} %get-tuple-element.22), channel_id=1, source_target_pairs={{0,28},{1,29},{2,30},{3,31},{4,0},{5,1},{6,2},{7,3},{8,4},{9,5},{1... | collective-permute-start | bytes 331784 | tf_op jit(solution)/shard_map/ppermute | solution.py:17
  53.5 7.8 %collective-permute-start.10 = (bf16[9,288,16]{1,2,0:T(8,128)(2,1)S(1)}, bf16[9,288,16]{1,2,0:T(8,128)(2,1)S(1)}, u32[]{:S(2)}, u32[]{:S(2)}) collective-permute-start(bf16[9,288,16]{1,2,0:T(8,128)(2,1)S(1)} %copy.19), channel_id=1, source_target_pairs={{0,1},{1,2},{2,3},{3,4},{4,5},{5,6},{6,7},{7,8},{8,9},{9,10},{10,1... | collective-permute-start | bytes 248840 | tf_op jit(solution)/shard_map/ppermute | solution.py:17
  54.7 7.9 %collective-permute-start.11 = (bf16[9,288,16]{1,2,0:T(8,128)(2,1)S(1)}, bf16[9,288,16]{1,2,0:T(8,128)(2,1)S(1)}, u32[]{:S(2)}, u32[]{:S(2)}) collective-permute-start(bf16[9,288,16]{1,2,0:T(8,128)(2,1)S(1)} %copy.20), channel_id=1, source_target_pairs={{0,31},{1,0},{2,1},{3,2},{4,3},{5,4},{6,5},{7,6},{8,7},{9,8},{10,9... | collective-permute-start | bytes 248840 | tf_op jit(solution)/shard_map/ppermute | solution.py:17
  151.0 14.3 %copy-start = (f32[272,400]{1,0:T(8,128)S(1)}, f32[272,400]{1,0:T(8,128)}, u32[]{:S(2)}) copy-start(f32[272,400]{1,0:T(8,128)} %broadcast_multiply_fusion.1) | copy-start | bytes 1305604
  175.2 2.0 copy-start.2
  257.2 22.4 %slice-start = ((s8[8388608]{0:T(1024)(128)(4,1)}), s8[4194304]{0:T(1024)(128)(4,1)S(1)}, s32[]{:S(2)}) async-start(s8[8388608]{0:T(1024)(128)(4,1)} %bitcast.42), calls=%async_computation | async-start | bytes 8388608
  268.7 10.9 %slice-start.1 = ((s8[8388608]{0:T(1024)(128)(4,1)}), s8[4194304]{0:T(1024)(128)(4,1)S(1)}, s32[]{:S(2)}) async-start(s8[8388608]{0:T(1024)(128)(4,1)} %bitcast.42), calls=%async_computation.1 | async-start | bytes 8388608
  268.7 10.9 %copy-start.1 = (f32[256,384]{1,0:T(8,128)S(1)}, f32[256,384]{1,0:T(8,128)}, u32[]{:S(2)}) copy-start(f32[256,384]{1,0:T(8,128)} %broadcast_multiply_fusion.2) | copy-start | bytes 1179652
  279.6 7.4 %copy-start.3 = (f32[256,384]{1,0:T(8,128)S(1)}, f32[256,384]{1,0:T(8,128)}, u32[]{:S(2)}) copy-start(f32[256,384]{1,0:T(8,128)} %get-tuple-element.59) | copy-start | bytes 1179652
where the time goes:
time: 296 us; the launch traced here: 292 us
  other arithmetic  194 us (66%)
  local copies, waits for them, and re-layouts  47.4 us (16%)
  starting transfers between devices  31.8 us (11%)
  waiting for transfers between devices  12.1 us (4%)
  matrix products  5.39 us (2%)
    add x12, other arithmetic, window_sum(): lax.slice_in_dim(partial_value, 0, extent - stride, axis=along_axis)  130 us
    slice x4, local copies, waits for them, and re-layouts, window_sum(): lax.slice_in_dim(partial_value, 0, extent - stride, axis=along_axis)  44.5 us
    ppermute x12, starting transfers between devices, passed_along(): return lax.ppermute(value, axis, pairs)  31.8 us
    add x2, other arithmetic, window_sum(): result = addend if result is None else result + addend  18.7 us
    ppermute x12, waiting for transfers between devices, passed_along(): return lax.ppermute(value, axis, pairs)  12.1 us
    div x1, other arithmetic, fit_gain(): box_means = box_sum(stacked, RADIUS) / coverage_map[None]  9.88 us
    div x1, other arithmetic, local(): smooth = box_sum(fitted_wide, RADIUS) / coverage_map[None]  7.38 us
  transfers between devices with their start and end apart: 12, of which 5 were waited for; matrix products, arithmetic and copies ran while one was open for 4% of the time, Pallas kernels for 0%

commit v1 on v0

v1 whole, which is shorter than its diff:
```python
import functools

import jax
import jax.numpy as jnp
from jax import lax
from jax.experimental import pallas as pl
from jax.experimental.pallas import tpu as pltpu
from jax.sharding import PartitionSpec as P

HALO = 32
MHALO = 8
RADIUS = 8
EPSILON = 0.1
GRID_COLS = 4
EDGE = 2 * RADIUS
LANES = 128
MESH = pl.DeviceIdType.MESH

STEPS = ((1, 0), (-1, 0), (0, 1), (0, -1), (1, 1), (1, -1), (-1, 1), (-1, -1))


def cubic_weights(fraction):
    squared = fraction * fraction
    cubed = squared * fraction
    return (
        -0.5 * cubed + squared - 0.5 * fraction,
        1.5 * cubed - 2.5 * squared + 1.0,
        -1.5 * cubed + 2.0 * squared + 0.5 * fraction,
        0.5 * cubed - 0.5 * squared,
    )


def band(taps, fraction, length, shift):
    weights = cubic_weights(fraction)
    outputs = taps.shape[1]
    distance = lax.broadcasted_iota(jnp.int32, (length, outputs), 0) - (taps + shift)
    matrix = jnp.zeros((length, outputs), jnp.float32)
    for offset in range(4):
        matrix = jnp.where(distance == offset, weights[offset], matrix)
    return matrix.astype(jnp.bfloat16)


def dot(left, right):
    return jnp.dot(left, right, preferred_element_type=jnp.float32)


def dot_t(left, right):
    return lax.dot_general(
        left, right, (((0,), (0,)), ((), ())), preferred_element_type=jnp.float32
    )


def place(sec_count, tile_count):
    total = sec_count * tile_count
    me = lax.axis_index("sec") * tile_count + lax.axis_index("tile")
    return lax.rem(me + 2, total), total


def resample_kernel(
    sec_count,
    tile_count,
    pan,
    ms,
    row_tap,
    row_frac,
    col_tap,
    col_frac,
    ms_row_tap,
    ms_row_frac,
    ms_col_tap,
    ms_col_frac,
    wide,
    pan_patch,
    ms_side,
    ms_vert,
    ms_corner,
    pack_east,
    pack_west,
    got_west,
    got_east,
    local_sem,
    send_pan,
    recv_pan,
    send_ms,
    recv_ms,
    send_edge,
    recv_edge,
):
    rows, cols = pan.shape
    bands, ms_rows, ms_cols = ms.shape
    channels = bands + 1
    placed, total = place(sec_count, tile_count)
    column = lax.rem(placed, GRID_COLS)
    grid_row = placed // GRID_COLS
    north_ok = grid_row > 0
    south_ok = grid_row < total // GRID_COLS - 1
    west_ok = column > 0
    east_ok = column < GRID_COLS - 1

    def device(down, right):
        there = lax.rem(placed + down * GRID_COLS + right - 2 + 2 * total, total)
        return (there // tile_count, lax.rem(there, tile_count))

    barrier = pltpu.get_barrier_semaphore()
    for down, right in STEPS:
        pl.semaphore_signal(
            barrier, inc=1, device_id=device(down, right), device_id_type=MESH
        )
    own = pltpu.make_async_copy(
        pan, pan_patch.at[HALO : HALO + rows, LANES : LANES + cols], local_sem
    )
    own.start()
    pl.semaphore_wait(barrier, len(STEPS))

    def span(step, size, depth):
        if step > 0:
            return slice(size - depth, size), slice(0, depth)
        if step < 0:
            return slice(0, depth), slice(depth + size, 2 * depth + size)
        return slice(0, size), slice(depth, depth + size)

    copies = []
    for index, (down, right) in enumerate(STEPS):
        row_from, row_to = span(down, rows, HALO)
        col_from, col_to = span(right, cols, LANES)
        copies.append(
            pltpu.make_async_remote_copy(
                src_ref=pan.at[row_from, col_from],
                dst_ref=pan_patch.at[row_to, col_to],
                send_sem=send_pan.at[index],
                recv_sem=recv_pan.at[index],
                device_id=device(down, right),
                device_id_type=MESH,
            )
        )
        if down == 0:
            source, target = ms, ms_side.at[0 if right > 0 else 1]
        else:
            source = ms.at[:, slice(ms_rows - 16, ms_rows) if down > 0 else slice(0, 16), :]
            if right == 0:
                target = ms_vert.at[0 if down > 0 else 1]
            else:
                target = ms_corner.at[(0 if right > 0 else 1) + (0 if down > 0 else 2)]
        copies.append(
            pltpu.make_async_remote_copy(
                src_ref=source,
                dst_ref=target,
                send_sem=send_ms.at[index],
                recv_sem=recv_ms.at[index],
                device_id=device(down, right),
                device_id_type=MESH,
            )
        )
    for copy in copies:
        copy.start()

    row_matrix = band(row_tap[...], row_frac[...], 2 * HALO + rows, 0)
    col_matrix = band(col_tap[...], col_frac[...], 2 * LANES + cols, LANES - HALO)
    ms_row_matrix = band(ms_row_tap[...], ms_row_frac[...], 32 + ms_rows, 16 - MHALO)
    ms_own_matrix = band(ms_col_tap[...], ms_col_frac[...], ms_cols, -MHALO)
    ms_west_matrix = band(ms_col_tap[...], ms_col_frac[...], ms_cols, ms_cols - MHALO)
    ms_east_matrix = band(ms_col_tap[...], ms_col_frac[...], ms_cols, -MHALO - ms_cols)

    own.wait()
    for copy in copies:
        copy.wait()

    def clear(ok, ref):
        @pl.when(jnp.logical_not(ok))
        def _():
            ref[...] = jnp.zeros(ref.shape, ref.dtype)

    clear(north_ok, pan_patch.at[:HALO, :])
    clear(south_ok, pan_patch.at[HALO + rows :, :])
    clear(west_ok, pan_patch.at[:, :LANES])
    clear(east_ok, pan_patch.at[:, LANES + cols :])
    clear(north_ok, ms_vert.at[0])
    clear(south_ok, ms_vert.at[1])
    clear(west_ok, ms_side.at[0])
    clear(east_ok, ms_side.at[1])
    for index, ok in enumerate(
        (north_ok & west_ok, north_ok & east_ok, south_ok & west_ok, south_ok & east_ok)
    ):
        clear(ok, ms_corner.at[index])

    segment = dot_t(row_matrix, pan_patch[...]).astype(jnp.bfloat16)
    wide[0, EDGE : EDGE + rows, :cols] = dot(segment, col_matrix).astype(jnp.bfloat16)
    for b in range(bands):
        parts = []
        for north, middle, south, matrix in (
            (ms_vert[0, b], ms[b], ms_vert[1, b], ms_own_matrix),
            (ms_corner[0, b], ms_side[0, b], ms_corner[2, b], ms_west_matrix),
            (ms_corner[1, b], ms_side[1, b], ms_corner[3, b], ms_east_matrix),
        ):
            block = jnp.concatenate([north, middle, south], axis=0)
            segment = dot_t(ms_row_matrix, block).astype(jnp.bfloat16)
            parts.append(dot(segment, matrix))
        wide[b + 1, EDGE : EDGE + rows, :cols] = (parts[0] + parts[1] + parts[2]).astype(
            jnp.bfloat16
        )

    lane = lax.broadcasted_iota(jnp.int32, (LANES, 2 * LANES), 0)
    slot = lax.broadcasted_iota(jnp.int32, (LANES, 2 * LANES), 1)
    east_sum = jnp.zeros((rows, 2 * LANES), jnp.float32)
    west_sum = jnp.zeros((rows, 2 * LANES), jnp.float32)
    for c in range(channels):
        pick = slot - c * EDGE
        inside = (pick >= 0) & (pick < EDGE)
        last = jnp.where(inside & (lane - (LANES - EDGE) == pick), 1.0, 0.0).astype(jnp.bfloat16)
        first = jnp.where(inside & (lane == pick), 1.0, 0.0).astype(jnp.bfloat16)
        east_sum = east_sum + dot(wide[c, EDGE : EDGE + rows, cols - LANES : cols], last)
        west_sum = west_sum + dot(wide[c, EDGE : EDGE + rows, :LANES], first)
    pack_east[...] = east_sum.astype(jnp.bfloat16)
    pack_west[...] = west_sum.astype(jnp.bfloat16)

    copies = []
    for index, (down, right) in enumerate(STEPS):
        row_from, row_to = span(down, rows, EDGE)
        if right == 0:
            source = wide.at[:, slice(row_from.start + EDGE, row_from.stop + EDGE), :cols]
            target = wide.at[:, row_to, :cols]
        elif right > 0:
            source, target = pack_east.at[row_from, :], got_west.at[row_to, :]
        else:
            source, target = pack_west.at[row_from, :], got_east.at[row_to, :]
        copies.append(
            pltpu.make_async_remote_copy(
                src_ref=source,
                dst_ref=target,
                send_sem=send_edge.at[index],
                recv_sem=recv_edge.at[index],
                device_id=device(down, right),
                device_id_type=MESH,
            )
        )
    for copy in copies:
        copy.start()
    for copy in copies:
        copy.wait()

    clear(north_ok, wide.at[:, :EDGE, :cols])
    clear(south_ok, wide.at[:, EDGE + rows :, :cols])
    for got, ok in ((got_west, west_ok), (got_east, east_ok)):
        clear(ok, got)
        clear(north_ok, got.at[:EDGE, :])
        clear(south_ok, got.at[EDGE + rows :, :])
    source = lax.broadcasted_iota(jnp.int32, (2 * LANES, LANES), 0)
    lane = lax.broadcasted_iota(jnp.int32, (2 * LANES, LANES), 1)
    for c in range(channels):
        pick = source - c * EDGE
        inside = (pick >= 0) & (pick < EDGE)
        from_east = jnp.where(inside & (lane == pick), 1.0, 0.0).astype(jnp.bfloat16)
        from_west = jnp.where(inside & (lane - (LANES - EDGE) == pick), 1.0, 0.0).astype(
            jnp.bfloat16
        )
        wide[c, :, cols:] = (
            dot(got_east[...], from_east) + dot(got_west[...], from_west)
        ).astype(jnp.bfloat16)


def sum_down(values, kept):
    count = values.shape[0]
    total = values
    for shift in (1, 2, 4):
        total = total + pltpu.roll(total, count - shift, 0)
    return total[:kept] + total[8 : kept + 8] + values[16 : kept + 16]


def inverse_cover(first, shape, axis, extent, kept):
    line = lax.broadcasted_iota(jnp.int32, shape, axis)
    places = line + first
    highest = jnp.minimum(places + RADIUS, extent - 1)
    lowest = jnp.maximum(places - RADIUS, 0)
    inside = (places >= 0) & (places < extent) & (line < kept)
    cover = jnp.where(inside, highest - lowest + 1, 1).astype(jnp.float32)
    return jnp.where(inside, 1.0 / cover, 0.0)


def filter_kernel(
    sec_count,
    tile_count,
    guide,
    bandref,
    out,
    box_a,
    box_b,
    inverse,
    inverse_out,
    mean_guide,
    inverse_var,
    sums_a,
    sums_b,
    fit_a,
    fit_b,
):
    wide_rows, width = guide.shape[1:]
    rows, cols = out.shape[1:]
    fit_rows = rows + EDGE
    chunks = width // LANES

    def box_across(values, matrix):
        high = values.astype(jnp.bfloat16)
        low = (values - high.astype(jnp.float32)).astype(jnp.bfloat16)
        return dot(high, matrix) + dot(low, matrix)

    @pl.when(pl.program_id(0) == 0)
    def _():
        placed, total = place(sec_count, tile_count)
        column = lax.rem(placed, GRID_COLS)
        grid_row = placed // GRID_COLS
        map_rows = total // GRID_COLS * rows
        map_cols = GRID_COLS * cols
        k = lax.broadcasted_iota(jnp.int32, (width, width), 0)
        j = lax.broadcasted_iota(jnp.int32, (width, width), 1)
        back = j - k
        back = jnp.where(back < 0, back + width, back)
        box_a[...] = jnp.where(back <= EDGE, 1.0, 0.0).astype(jnp.bfloat16)
        k = lax.broadcasted_iota(jnp.int32, (width, cols), 0)
        j = lax.broadcasted_iota(jnp.int32, (width, cols), 1)
        box_b[...] = jnp.where((k >= j) & (k - j <= EDGE), 1.0, 0.0).astype(jnp.bfloat16)
        row0 = grid_row * rows
        col0 = column * cols
        inverse[...] = inverse_cover(
            row0 - RADIUS, (fit_rows, width), 0, map_rows, fit_rows
        ) * inverse_cover(col0 - RADIUS, (fit_rows, width), 1, map_cols, cols + EDGE)
        inverse_out[...] = inverse_cover(row0, (rows, cols), 0, map_rows, rows) * inverse_cover(
            col0, (rows, cols), 1, map_cols, cols
        )
        own = guide[0].astype(jnp.float32)
        sums_a[...] = dot(guide[0], box_a[...])
        sums_b[...] = box_across(own * own, box_a[...])
        for t in range(chunks):
            lanes = slice(t * LANES, (t + 1) * LANES)
            scale = inverse[:, lanes]
            mean = sum_down(sums_a[:, lanes], fit_rows) * scale
            square = sum_down(sums_b[:, lanes], fit_rows) * scale
            mean_guide[:, lanes] = mean
            inverse_var[:, lanes] = 1.0 / (square - mean * mean + EPSILON)

    sums_a[...] = dot(bandref[0], box_a[...])
    sums_b[...] = box_across(
        guide[0].astype(jnp.float32) * bandref[0].astype(jnp.float32), box_a[...]
    )
    for t in range(chunks):
        lanes = slice(t * LANES, (t + 1) * LANES)
        scale = inverse[:, lanes]
        mean = mean_guide[:, lanes]
        mean_band = sum_down(sums_a[:, lanes], fit_rows) * scale
        cross = sum_down(sums_b[:, lanes], fit_rows) * scale
        gain = (cross - mean * mean_band) * inverse_var[:, lanes]
        fit_a[:, lanes] = gain.astype(jnp.bfloat16)
        fit_b[:, lanes] = (mean_band - gain * mean).astype(jnp.bfloat16)
    sums_a[:fit_rows, :cols] = dot(fit_a[...], box_b[...])
    sums_b[:fit_rows, :cols] = dot(fit_b[...], box_b[...])
    for t in range(cols // LANES):
        lanes = slice(t * LANES, (t + 1) * LANES)
        own = guide[0, EDGE : EDGE + rows, lanes].astype(jnp.float32)
        gain = sum_down(sums_a[:fit_rows, lanes], rows)
        offset = sum_down(sums_b[:fit_rows, lanes], rows)
        out[0, :, lanes] = ((gain * own + offset) * inverse_out[:, lanes]).astype(jnp.bfloat16)


def local(sec_count, tile_count, pan_source, ms_source, *tables):
    rows, cols = pan_source.shape[1:]
    bands, _, ms_rows, ms_cols = ms_source.shape
    channels = bands + 1
    wide_rows = rows + 2 * EDGE
    width = cols + LANES
    bf16, f32 = jnp.bfloat16, jnp.float32
    vmem = pl.BlockSpec(memory_space=pltpu.VMEM)
    dma = pltpu.SemaphoreType.DMA
    wide = pl.pallas_call(
        functools.partial(resample_kernel, sec_count, tile_count),
        out_shape=jax.ShapeDtypeStruct((channels, wide_rows, width), bf16),
        in_specs=[vmem] * (2 + len(tables)),
        out_specs=vmem,
        scratch_shapes=[
            pltpu.VMEM((rows + 2 * HALO, cols + 2 * LANES), bf16),
            pltpu.VMEM((2, bands, ms_rows, ms_cols), bf16),
            pltpu.VMEM((2, bands, 16, ms_cols), bf16),
            pltpu.VMEM((4, bands, 16, ms_cols), bf16),
            pltpu.VMEM((rows, 2 * LANES), bf16),
            pltpu.VMEM((rows, 2 * LANES), bf16),
            pltpu.VMEM((wide_rows, 2 * LANES), bf16),
            pltpu.VMEM((wide_rows, 2 * LANES), bf16),
            dma,
        ]
        + [dma((len(STEPS),))] * 6,
        compiler_params=pltpu.CompilerParams(
            collective_id=0, has_side_effects=True, vmem_limit_bytes=48 * 2**20
        ),
    )(pan_source.reshape(rows, cols), ms_source.reshape(bands, ms_rows, ms_cols), *tables)
    fit_rows = rows + EDGE
    sharpened = pl.pallas_call(
        functools.partial(filter_kernel, sec_count, tile_count),
        grid=(bands,),
        out_shape=jax.ShapeDtypeStruct((bands, rows, cols), bf16),
        in_specs=[
            pl.BlockSpec((1, wide_rows, width), lambda b: (0, 0, 0)),
            pl.BlockSpec((1, wide_rows, width), lambda b: (b + 1, 0, 0)),
        ],
        out_specs=pl.BlockSpec((1, rows, cols), lambda b: (b, 0, 0)),
        scratch_shapes=[
            pltpu.VMEM((width, width), bf16),
            pltpu.VMEM((width, cols), bf16),
            pltpu.VMEM((fit_rows, width), f32),
            pltpu.VMEM((rows, cols), f32),
            pltpu.VMEM((fit_rows, width), f32),
            pltpu.VMEM((fit_rows, width), f32),
            pltpu.VMEM((wide_rows, width), f32),
            pltpu.VMEM((wide_rows, width), f32),
            pltpu.VMEM((fit_rows, width), bf16),
            pltpu.VMEM((fit_rows, width), bf16),
        ],
        compiler_params=pltpu.CompilerParams(vmem_limit_bytes=48 * 2**20),
    )(wide, wide)
    return sharpened[:, None]


def solution(mesh):
    tiles = ("sec", "tile")
    table = P(tiles, None)
    return jax.shard_map(
        functools.partial(local, mesh.shape["sec"], mesh.shape["tile"]),
        mesh=mesh,
        in_specs=(P(tiles, None, None), P(None, tiles, None, None)) + (table,) * 8,
        out_specs=P(None, tiles, None, None),
        check_vma=False,
    )
```

time: 296 us -> 66.3 us (0.22); the launches traced: 292 us -> 66 us
  other arithmetic: 194 us -> 0 us
  Pallas kernels: 0 us -> 58.7 us
  local copies, waits for them, and re-layouts: 47.4 us -> 7.26 us
  starting transfers between devices: 31.8 us -> 0 us
  waiting for transfers between devices: 12.1 us -> 0 us
  matrix products: 5.39 us -> 0 us
    add x18 -> x0, other arithmetic: 150 us -> none  [the longest x12 130 us: window_sum(): lax.slice_in_dim(partial_value, 0, extent - stride, axis=along_axis)]
    pallas_call x0 -> x2, Pallas kernels: none -> 58.7 us  [the longest x1 43.5 us: local(): pl.pallas_call(functools.partial(resample_kernel, sec_count, tile_count),...]
    slice x9 -> x0, local copies, waits for them, and re-layouts: 46.7 us -> none  [the longest x4 44.5 us: window_sum(): lax.slice_in_dim(partial_value, 0, extent - stride, axis=along_axis)]
    ppermute x12 -> x0, starting transfers between devices: 31.8 us -> none  [passed_along(): return lax.ppermute(value, axis, pairs)]
    div x3 -> x0, other arithmetic: 17.4 us -> none  [the longest x1 9.88 us: fit_gain(): box_means = box_sum(stacked, RADIUS) / coverage_map[None]]
    ppermute x12 -> x0, waiting for transfers between devices: 12.1 us -> none  [passed_along(): return lax.ppermute(value, axis, pairs)]
    convert_element_type x7 -> x0, other arithmetic: 7.87 us -> none  [the longest x1 4.74 us: local(): fitted_wide = lax.optimization_barrier(fitted).astype(jnp.float32)]
    unnamed x12 -> x20, local copies, waits for them, and re-layouts: 0.02 us -> 7.26 us
  transfers between devices with their start and end apart: 12 -> 0, of which waited for: 5 -> 0; matrix products, arithmetic and copies ran while one was open for 4% -> 0% of each run, Pallas kernels for 0% -> 0%
where the time goes in v1:
time: 66.3 us; the launch traced here: 66 us
  Pallas kernels  58.7 us (89%)
  local copies, waits for them, and re-layouts  7.26 us (11%)
    pallas_call x1, Pallas kernels, local(): pl.pallas_call(functools.partial(resample_kernel, sec_count, tile_count),...  43.5 us
    pallas_call x1, Pallas kernels, local(): pl.pallas_call(functools.partial(filter_kernel, sec_count, tile_count), g...  15.3 us
    unnamed x20, local copies, waits for them, and re-layouts  7.26 us

profile of v1, /device:TPU:0, one launch (start us, length us, event | category | flops | bytes accessed | tf_op | source)
XLA Modules:
  0.0 66.0 jit_solution(13996559707562381573)
XLA Ops:
  0.0 0.0 copy-start
  0.0 0.9 %copy-done = bf16[1,256,384]{2,1,0:T(8,128)(2,1)S(1)} copy-done((bf16[1,256,384]{2,1,0:T(8,128)(2,1)S(1)}, bf16[1,256,384]{2,1,0:T(8,128)(2,1)}, u32[]{:S(2)}) %copy-start) | copy-done | bytes 196632
  0.9 0.0 copy-start.1
  0.9 0.9 %copy-done.1 = bf16[8,1,64,96]{3,2,1,0:T(8,128)(2,1)S(1)} copy-done((bf16[8,1,64,96]{3,2,1,0:T(8,128)(2,1)S(1)}, bf16[8,1,64,96]{3,2,1,0:T(8,128)(2,1)}, u32[]{:S(2)}) %copy-start.1) | copy-done | bytes 98328
  1.8 0.0 copy-start.2
  1.8 0.7 %copy-done.2 = s32[1,384]{1,0:T(1,128)S(1)} copy-done((s32[1,384]{1,0:T(1,128)S(1)}, s32[1,384]{1,0:T(1,128)}, u32[]{:S(2)}) %copy-start.2) | copy-done | bytes 1560
  2.5 0.0 copy-start.3
  2.5 0.7 %copy-done.3 = f32[1,384]{1,0:T(1,128)S(1)} copy-done((f32[1,384]{1,0:T(1,128)S(1)}, f32[1,384]{1,0:T(1,128)}, u32[]{:S(2)}) %copy-start.3) | copy-done | bytes 1560
  3.2 0.0 copy-start.4
  3.2 0.7 %copy-done.4 = s32[1,384]{1,0:T(1,128)S(1)} copy-done((s32[1,384]{1,0:T(1,128)S(1)}, s32[1,384]{1,0:T(1,128)}, u32[]{:S(2)}) %copy-start.4) | copy-done | bytes 1560
  3.9 0.0 copy-start.5
  3.9 0.7 %copy-done.5 = f32[1,384]{1,0:T(1,128)S(1)} copy-done((f32[1,384]{1,0:T(1,128)S(1)}, f32[1,384]{1,0:T(1,128)}, u32[]{:S(2)}) %copy-start.5) | copy-done | bytes 1560
  4.6 0.0 copy-start.6
  4.6 0.7 %copy-done.6 = s32[1,256]{1,0:T(1,128)S(1)} copy-done((s32[1,256]{1,0:T(1,128)S(1)}, s32[1,256]{1,0:T(1,128)}, u32[]{:S(2)}) %copy-start.6) | copy-done | bytes 1048
  5.2 0.0 copy-start.7
  5.2 0.7 %copy-done.7 = f32[1,256]{1,0:T(1,128)S(1)} copy-done((f32[1,256]{1,0:T(1,128)S(1)}, f32[1,256]{1,0:T(1,128)}, u32[]{:S(2)}) %copy-start.7) | copy-done | bytes 1048
  5.9 0.0 copy-start.8
  5.9 0.7 %copy-done.8 = s32[1,256]{1,0:T(1,128)S(1)} copy-done((s32[1,256]{1,0:T(1,128)S(1)}, s32[1,256]{1,0:T(1,128)}, u32[]{:S(2)}) %copy-start.8) | copy-done | bytes 1048
  6.6 0.0 copy-start.9
  6.6 0.7 %copy-done.9 = f32[1,256]{1,0:T(1,128)S(1)} copy-done((f32[1,256]{1,0:T(1,128)S(1)}, f32[1,256]{1,0:T(1,128)}, u32[]{:S(2)}) %copy-start.9) | copy-done | bytes 1048
  7.3 43.5 %shard_map.100.guide.bandref = bf16[9,288,512]{2,1,0:T(8,128)(2,1)S(1)} custom-call(bf16[256,384]{1,0:T(8,128)(2,1)S(1)} %bitcast.5, bf16[8,64,96]{2,1,0:T(8,128)(2,1)S(1)} %bitcast.6, s32[1,256]{1,0:T(1,128)S(1)} %copy-done.6, f32[1,256]{1,0:T(1,128)S(1)} %copy-done.7, s32[1,384]{1,0:T(1,128)S(1)} %copy-done.2, f32[1,384]{1,0:T(1,128)S(1)} %copy-done.3, ...), custom_call_target="tpu_custom_call" | custom-call | tf_op jit(solution)/shard_map/pallas_call | solution.py:372
  50.7 15.3 %shard_map.101 = bf16[8,256,384]{2,1,0:T(8,128)(2,1)} custom-call(bf16[9,288,512]{2,1,0:T(8,128)(2,1)S(1)} %shard_map.100.guide.bandref, bf16[9,288,512]{2,1,0:T(8,128)(2,1)S(1)} %shard_map.100.guide.bandref), custom_call_target="tpu_custom_call" | custom-call | tf_op jit(solution)/shard_map/pallas_call | solution.py:394
Async XLA Ops:
  0.0 0.9 %copy-start = (bf16[1,256,384]{2,1,0:T(8,128)(2,1)S(1)}, bf16[1,256,384]{2,1,0:T(8,128)(2,1)}, u32[]{:S(2)}) copy-start(bf16[1,256,384]{2,1,0:T(8,128)(2,1)} %param.10) | copy-start | bytes 589828
  0.9 0.9 %copy-start.1 = (bf16[8,1,64,96]{3,2,1,0:T(8,128)(2,1)S(1)}, bf16[8,1,64,96]{3,2,1,0:T(8,128)(2,1)}, u32[]{:S(2)}) copy-start(bf16[8,1,64,96]{3,2,1,0:T(8,128)(2,1)} %param.11) | copy-start | bytes 294916
  1.8 0.7 %copy-start.2 = (s32[1,384]{1,0:T(1,128)S(1)}, s32[1,384]{1,0:T(1,128)}, u32[]{:S(2)}) copy-start(s32[1,384]{1,0:T(1,128)} %col_tap.1) | copy-start | bytes 4612
  2.5 0.7 %copy-start.3 = (f32[1,384]{1,0:T(1,128)S(1)}, f32[1,384]{1,0:T(1,128)}, u32[]{:S(2)}) copy-start(f32[1,384]{1,0:T(1,128)} %col_frac.1) | copy-start | bytes 4612
  3.2 0.7 %copy-start.4 = (s32[1,384]{1,0:T(1,128)S(1)}, s32[1,384]{1,0:T(1,128)}, u32[]{:S(2)}) copy-start(s32[1,384]{1,0:T(1,128)} %ms_col_tap.1) | copy-start | bytes 4612
  3.9 0.7 %copy-start.5 = (f32[1,384]{1,0:T(1,128)S(1)}, f32[1,384]{1,0:T(1,128)}, u32[]{:S(2)}) copy-start(f32[1,384]{1,0:T(1,128)} %ms_col_frac.1) | copy-start | bytes 4612
  4.6 0.7 %copy-start.6 = (s32[1,256]{1,0:T(1,128)S(1)}, s32[1,256]{1,0:T(1,128)}, u32[]{:S(2)}) copy-start(s32[1,256]{1,0:T(1,128)} %row_tap.1) | copy-start | bytes 3076
  5.2 0.7 %copy-start.7 = (f32[1,256]{1,0:T(1,128)S(1)}, f32[1,256]{1,0:T(1,128)}, u32[]{:S(2)}) copy-start(f32[1,256]{1,0:T(1,128)} %row_frac.1) | copy-start | bytes 3076
  5.9 0.7 %copy-start.8 = (s32[1,256]{1,0:T(1,128)S(1)}, s32[1,256]{1,0:T(1,128)}, u32[]{:S(2)}) copy-start(s32[1,256]{1,0:T(1,128)} %ms_row_tap.1) | copy-start | bytes 3076
  6.6 0.7 %copy-start.9 = (f32[1,256]{1,0:T(1,128)S(1)}, f32[1,256]{1,0:T(1,128)}, u32[]{:S(2)}) copy-start(f32[1,256]{1,0:T(1,128)} %ms_row_frac.1) | copy-start | bytes 3076

commit v2 on v1

--- a/solution.py
+++ b/solution.py
@@ -31,13 +31,24 @@
 
 
 def band(taps, fraction, length, shift):
+    line = lax.broadcasted_iota(jnp.int32, (length, taps.shape[1]), 0)
+    return band_at(line - shift, taps, fraction)
+
+
+def band_at(position, taps, fraction):
     weights = cubic_weights(fraction)
-    outputs = taps.shape[1]
-    distance = lax.broadcasted_iota(jnp.int32, (length, outputs), 0) - (taps + shift)
-    matrix = jnp.zeros((length, outputs), jnp.float32)
+    distance = position - taps
+    matrix = jnp.zeros(position.shape, jnp.float32)
     for offset in range(4):
         matrix = jnp.where(distance == offset, weights[offset], matrix)
     return matrix.astype(jnp.bfloat16)
+
+
+def picker(shape, shift, low, high):
+    source = lax.broadcasted_iota(jnp.int32, shape, 0)
+    target = lax.broadcasted_iota(jnp.int32, shape, 1)
+    chosen = (target - source == shift) & (source >= low) & (source < high)
+    return jnp.where(chosen, 1.0, 0.0).astype(jnp.bfloat16)
 
 
 def dot(left, right):
@@ -70,15 +81,27 @@
     ms_col_tap,
     ms_col_frac,
     wide,
+    ms_own,
+    row_tap_here,
+    row_frac_here,
+    col_tap_here,
+    col_frac_here,
+    ms_row_tap_here,
+    ms_row_frac_here,
+    ms_col_tap_here,
+    ms_col_frac_here,
     pan_patch,
-    ms_side,
     ms_vert,
-    ms_corner,
+    pan_pack,
+    pan_got,
+    ms_pack,
+    ms_got,
     pack_east,
     pack_west,
     got_west,
     got_east,
     local_sem,
+    table_sem,
     send_pan,
     recv_pan,
     send_ms,
@@ -101,16 +124,87 @@
         there = lax.rem(placed + down * GRID_COLS + right - 2 + 2 * total, total)
         return (there // tile_count, lax.rem(there, tile_count))
 
+    def reaches(down, right):
+        ok = True
+        if down:
+            ok = south_ok if down > 0 else north_ok
+        if right:
+            side = east_ok if right > 0 else west_ok
+            ok = side if ok is True else ok & side
+        return ok
+
+    def start_all(steps, copies):
+        for (down, right), copy in zip(steps, copies):
+            pl.when(reaches(down, right))(copy.start)
+
+    def wait_all(steps, copies):
+        for (down, right), copy in zip(steps, copies):
+            pl.when(reaches(-down, -right))(copy.wait_recv)
+        for (down, right), copy in zip(steps, copies):
+            pl.when(reaches(down, right))(copy.wait_send)
+
     barrier = pltpu.get_barrier_semaphore()
     for down, right in STEPS:
-        pl.semaphore_signal(
-            barrier, inc=1, device_id=device(down, right), device_id_type=MESH
-        )
+
+        @pl.when(reaches(down, right))
+        def _(down=down, right=right):
+            pl.semaphore_signal(
+                barrier, inc=1, device_id=device(down, right), device_id_type=MESH
+            )
+
     own = pltpu.make_async_copy(
         pan, pan_patch.at[HALO : HALO + rows, LANES : LANES + cols], local_sem
     )
+    fetched = [
+        pltpu.make_async_copy(source, target, table_sem.at[index])
+        for index, (source, target) in enumerate(
+            (
+                (row_tap, row_tap_here),
+                (row_frac, row_frac_here),
+                (col_tap, col_tap_here),
+                (col_frac, col_frac_here),
+                (ms_row_tap, ms_row_tap_here),
+                (ms_row_frac, ms_row_frac_here),
+                (ms_col_tap, ms_col_tap_here),
+                (ms_col_frac, ms_col_frac_here),
+                (ms, ms_own),
+            )
+        )
+    ]
+    for copy in fetched:
+        copy.start()
     own.start()
-    pl.semaphore_wait(barrier, len(STEPS))
+    for copy in fetched:
+        copy.wait()
+    own.wait()
+    group = rows // (LANES // HALO)
+    ms_slot = LANES // 2
+    for side in range(2):
+        total_pan = jnp.zeros((group, LANES), jnp.float32)
+        first_lane = 0 if side else LANES - HALO
+        block = slice(LANES, 2 * LANES) if side else slice(cols, cols + LANES)
+        for g in range(LANES // HALO):
+            move = picker(
+                (LANES, LANES), g * HALO - first_lane, first_lane, first_lane + HALO
+            )
+            lines = slice(HALO + g * group, HALO + (g + 1) * group)
+            total_pan = total_pan + dot(pan_patch[lines, block], move)
+        pan_pack[side] = total_pan.astype(jnp.bfloat16)
+        total_ms = jnp.zeros((ms_rows, LANES), jnp.float32)
+        first_lane = 0 if side else ms_cols - MHALO
+        for b in range(bands):
+            move = picker(
+                (ms_cols, LANES),
+                side * ms_slot + b * MHALO - first_lane,
+                first_lane,
+                first_lane + MHALO,
+            )
+            total_ms = total_ms + dot(ms_own[b], move)
+        ms_pack[side] = total_ms.astype(jnp.bfloat16)
+
+    tall = 1 + north_ok.astype(jnp.int32) + south_ok.astype(jnp.int32)
+    broad = 1 + west_ok.astype(jnp.int32) + east_ok.astype(jnp.int32)
+    pl.semaphore_wait(barrier, tall * broad - 1)
 
     def span(step, size, depth):
         if step > 0:
@@ -119,28 +213,32 @@
             return slice(0, depth), slice(depth + size, 2 * depth + size)
         return slice(0, size), slice(depth, depth + size)
 
-    copies = []
+    steps, copies = [], []
     for index, (down, right) in enumerate(STEPS):
         row_from, row_to = span(down, rows, HALO)
         col_from, col_to = span(right, cols, LANES)
+        side = 0 if right > 0 else 1
+        if down:
+            source, target = pan.at[row_from, col_from], pan_patch.at[row_to, col_to]
+        else:
+            source, target = pan_pack.at[side], pan_got.at[side]
+        steps.append((down, right))
         copies.append(
             pltpu.make_async_remote_copy(
-                src_ref=pan.at[row_from, col_from],
-                dst_ref=pan_patch.at[row_to, col_to],
+                src_ref=source,
+                dst_ref=target,
                 send_sem=send_pan.at[index],
                 recv_sem=recv_pan.at[index],
                 device_id=device(down, right),
                 device_id_type=MESH,
             )
         )
-        if down == 0:
-            source, target = ms, ms_side.at[0 if right > 0 else 1]
+        row_from, row_to = span(down, ms_rows, 16)
+        if right:
+            source, target = ms_pack.at[side, row_from, :], ms_got.at[side, row_to, :]
         else:
-            source = ms.at[:, slice(ms_rows - 16, ms_rows) if down > 0 else slice(0, 16), :]
-            if right == 0:
-                target = ms_vert.at[0 if down > 0 else 1]
-            else:
-                target = ms_corner.at[(0 if right > 0 else 1) + (0 if down > 0 else 2)]
+            source, target = ms_own.at[:, row_from, :], ms_vert.at[0 if down > 0 else 1]
+        steps.append((down, right))
         copies.append(
             pltpu.make_async_remote_copy(
                 src_ref=source,
@@ -151,24 +249,36 @@
                 device_id_type=MESH,
             )
         )
-    for copy in copies:
-        copy.start()
-
-    row_matrix = band(row_tap[...], row_frac[...], 2 * HALO + rows, 0)
-    col_matrix = band(col_tap[...], col_frac[...], 2 * LANES + cols, LANES - HALO)
-    ms_row_matrix = band(ms_row_tap[...], ms_row_frac[...], 32 + ms_rows, 16 - MHALO)
-    ms_own_matrix = band(ms_col_tap[...], ms_col_frac[...], ms_cols, -MHALO)
-    ms_west_matrix = band(ms_col_tap[...], ms_col_frac[...], ms_cols, ms_cols - MHALO)
-    ms_east_matrix = band(ms_col_tap[...], ms_col_frac[...], ms_cols, -MHALO - ms_cols)
-
-    own.wait()
-    for copy in copies:
-        copy.wait()
+    start_all(steps, copies)
+    row_matrix = band(row_tap_here[...], row_frac_here[...], 2 * HALO + rows, 0)
+    col_matrix = band(col_tap_here[...], col_frac_here[...], 2 * LANES + cols, LANES - HALO)
+    ms_row_matrix = band(ms_row_tap_here[...], ms_row_frac_here[...], 32 + ms_rows, 16 - MHALO)
+    ms_col_taps = ms_col_tap_here[...]
+    ms_col_fracs = ms_col_frac_here[...]
+    ms_own_matrix = band(ms_col_taps, ms_col_fracs, ms_cols, -MHALO)
+    lane = lax.broadcasted_iota(jnp.int32, (LANES, cols), 0)
+    ms_halo_matrix = band_at(
+        jnp.where(lane < ms_slot, 0, ms_cols + MHALO) + lax.rem(lane, MHALO),
+        ms_col_taps,
+        ms_col_fracs,
+    )
+
+    wait_all(steps, copies)
 
     def clear(ok, ref):
         @pl.when(jnp.logical_not(ok))
         def _():
             ref[...] = jnp.zeros(ref.shape, ref.dtype)
+
+    clear(west_ok, pan_got.at[0])
+    clear(east_ok, pan_got.at[1])
+    for side in range(2):
+        first_lane = 0 if side else LANES - HALO
+        block = slice(LANES + cols, 2 * LANES + cols) if side else slice(0, LANES)
+        for g in range(LANES // HALO):
+            move = picker((LANES, LANES), first_lane - g * HALO, g * HALO, (g + 1) * HALO)
+            lines = slice(HALO + g * group, HALO + (g + 1) * group)
+            pan_patch[lines, block] = dot(pan_got[side], move).astype(jnp.bfloat16)
 
     clear(north_ok, pan_patch.at[:HALO, :])
     clear(south_ok, pan_patch.at[HALO + rows :, :])
@@ -176,28 +286,23 @@
     clear(east_ok, pan_patch.at[:, LANES + cols :])
     clear(north_ok, ms_vert.at[0])
     clear(south_ok, ms_vert.at[1])
-    clear(west_ok, ms_side.at[0])
-    clear(east_ok, ms_side.at[1])
-    for index, ok in enumerate(
-        (north_ok & west_ok, north_ok & east_ok, south_ok & west_ok, south_ok & east_ok)
-    ):
-        clear(ok, ms_corner.at[index])
+    for side, ok in ((0, west_ok), (1, east_ok)):
+        clear(ok, ms_got.at[side])
+        clear(north_ok, ms_got.at[side, :16, :])
+        clear(south_ok, ms_got.at[side, 16 + ms_rows :, :])
 
     segment = dot_t(row_matrix, pan_patch[...]).astype(jnp.bfloat16)
     wide[0, EDGE : EDGE + rows, :cols] = dot(segment, col_matrix).astype(jnp.bfloat16)
+    lane = lax.broadcasted_iota(jnp.int32, (rows, LANES), 1)
+    halo_segment = dot_t(ms_row_matrix, ms_got[0]) + dot_t(ms_row_matrix, ms_got[1])
+    halo_band = lax.rem(lane, ms_slot) // MHALO
     for b in range(bands):
-        parts = []
-        for north, middle, south, matrix in (
-            (ms_vert[0, b], ms[b], ms_vert[1, b], ms_own_matrix),
-            (ms_corner[0, b], ms_side[0, b], ms_corner[2, b], ms_west_matrix),
-            (ms_corner[1, b], ms_side[1, b], ms_corner[3, b], ms_east_matrix),
-        ):
-            block = jnp.concatenate([north, middle, south], axis=0)
-            segment = dot_t(ms_row_matrix, block).astype(jnp.bfloat16)
-            parts.append(dot(segment, matrix))
-        wide[b + 1, EDGE : EDGE + rows, :cols] = (parts[0] + parts[1] + parts[2]).astype(
-            jnp.bfloat16
-        )
+        block = jnp.concatenate([ms_vert[0, b], ms_own[b], ms_vert[1, b]], axis=0)
+        segment = dot_t(ms_row_matrix, block).astype(jnp.bfloat16)
+        beside = jnp.where(halo_band == b, halo_segment, 0.0).astype(jnp.bfloat16)
+        wide[b + 1, EDGE : EDGE + rows, :cols] = (
+            dot(segment, ms_own_matrix) + dot(beside, ms_halo_matrix)
+        ).astype(jnp.bfloat16)
 
     lane = lax.broadcasted_iota(jnp.int32, (LANES, 2 * LANES), 0)
     slot = lax.broadcasted_iota(jnp.int32, (LANES, 2 * LANES), 1)
@@ -233,10 +338,8 @@
                 device_id_type=MESH,
             )
         )
-    for copy in copies:
-        copy.start()
-    for copy in copies:
-        copy.wait()
+    start_all(STEPS, copies)
+    wait_all(STEPS, copies)
 
     clear(north_ok, wide.at[:, :EDGE, :cols])
     clear(south_ok, wide.at[:, EDGE + rows :, :cols])
@@ -372,23 +475,26 @@
     wide = pl.pallas_call(
         functools.partial(resample_kernel, sec_count, tile_count),
         out_shape=jax.ShapeDtypeStruct((channels, wide_rows, width), bf16),
-        in_specs=[vmem] * (2 + len(tables)),
+        in_specs=[pl.BlockSpec(memory_space=pltpu.HBM)] * (2 + len(tables)),
         out_specs=vmem,
-        scratch_shapes=[
+        scratch_shapes=[pltpu.VMEM((bands, ms_rows, ms_cols), bf16)]
+        + [pltpu.VMEM(table.shape, table.dtype) for table in tables]
+        + [
             pltpu.VMEM((rows + 2 * HALO, cols + 2 * LANES), bf16),
-            pltpu.VMEM((2, bands, ms_rows, ms_cols), bf16),
             pltpu.VMEM((2, bands, 16, ms_cols), bf16),
-            pltpu.VMEM((4, bands, 16, ms_cols), bf16),
+            pltpu.VMEM((2, rows * HALO // LANES, LANES), bf16),
+            pltpu.VMEM((2, rows * HALO // LANES, LANES), bf16),
+            pltpu.VMEM((2, ms_rows, LANES), bf16),
+            pltpu.VMEM((2, ms_rows + 32, LANES), bf16),
             pltpu.VMEM((rows, 2 * LANES), bf16),
             pltpu.VMEM((rows, 2 * LANES), bf16),
             pltpu.VMEM((wide_rows, 2 * LANES), bf16),
             pltpu.VMEM((wide_rows, 2 * LANES), bf16),
             dma,
+            dma((len(tables) + 1,)),
         ]
         + [dma((len(STEPS),))] * 6,
-        compiler_params=pltpu.CompilerParams(
-            collective_id=0, has_side_effects=True, vmem_limit_bytes=48 * 2**20
-        ),
+        compiler_params=pltpu.CompilerParams(collective_id=0, has_side_effects=True),
     )(pan_source.reshape(rows, cols), ms_source.reshape(bands, ms_rows, ms_cols), *tables)
     fit_rows = rows + EDGE
     sharpened = pl.pallas_call(
@@ -412,7 +518,6 @@
             pltpu.VMEM((fit_rows, width), bf16),
             pltpu.VMEM((fit_rows, width), bf16),
         ],
-        compiler_params=pltpu.CompilerParams(vmem_limit_bytes=48 * 2**20),
     )(wide, wide)
     return sharpened[:, None]
 

time: 66.3 us -> 48.6 us (0.73)
  the two profiles are of different devices: /device:TPU:0 before, /device:TPU:5 now
where the time goes in v2:
time: 48.6 us; the launch traced here: 48.5 us
  Pallas kernels  48.5 us (100%)
    pallas_call x1, Pallas kernels, local(): pl.pallas_call(functools.partial(resample_kernel, sec_count, tile_count),...  32.1 us
    pallas_call x1, Pallas kernels, local(): pl.pallas_call(functools.partial(filter_kernel, sec_count, tile_count), g...  16.3 us

profile of v2, /device:TPU:5, one launch (start us, length us, event | category | flops | bytes accessed | tf_op | source)
XLA Modules:
  0.0 48.5 jit_solution(12067063277400559597)
XLA Ops:
  0.0 32.1 %shard_map.100.guide.bandref = bf16[9,288,512]{2,1,0:T(8,128)(2,1)} custom-call(bf16[256,384]{1,0:T(8,128)(2,1)} %bitcast.5, bf16[8,64,96]{2,1,0:T(8,128)(2,1)} %bitcast.6, s32[1,256]{1,0:T(1,128)} %row_tap.1, f32[1,256]{1,0:T(1,128)} %row_frac.1, s32[1,384]{1,0:T(1,128)} %col_tap.1, f32[1,384]{1,0:T(1,128)} %col_frac.1, s32[1,256]{1,0:T(1,128)} %ms_row_tap.1, ...), custom_call_target="tpu_custom_call" | custom-call | tf_op jit(solution)/shard_map/pallas_call | solution.py:475
  32.1 16.3 %shard_map.101 = bf16[8,256,384]{2,1,0:T(8,128)(2,1)} custom-call(bf16[9,288,512]{2,1,0:T(8,128)(2,1)} %shard_map.100.guide.bandref, bf16[9,288,512]{2,1,0:T(8,128)(2,1)} %shard_map.100.guide.bandref), custom_call_target="tpu_custom_call" | custom-call | tf_op jit(solution)/shard_map/pallas_call | solution.py:500

commit v3 on v2

--- a/solution.py
+++ b/solution.py
@@ -92,6 +92,7 @@
     ms_col_frac_here,
     pan_patch,
     ms_vert,
+    ms_tall,
     pan_pack,
     pan_got,
     ms_pack,
@@ -108,6 +109,8 @@
     recv_ms,
     send_edge,
     recv_edge,
+    send_tall,
+    recv_tall,
 ):
     rows, cols = pan.shape
     bands, ms_rows, ms_cols = ms.shape
@@ -201,6 +204,10 @@
             )
             total_ms = total_ms + dot(ms_own[b], move)
         ms_pack[side] = total_ms.astype(jnp.bfloat16)
+        lines = slice(0, MHALO) if side else slice(ms_rows - MHALO, ms_rows)
+        for pair in range(bands // 2):
+            both = [ms_own[b].astype(jnp.float32)[lines] for b in (2 * pair, 2 * pair + 1)]
+            ms_tall[side, pair] = jnp.concatenate(both, axis=0).astype(jnp.bfloat16)
 
     tall = 1 + north_ok.astype(jnp.int32) + south_ok.astype(jnp.int32)
     broad = 1 + west_ok.astype(jnp.int32) + east_ok.astype(jnp.int32)
@@ -237,7 +244,7 @@
         if right:
             source, target = ms_pack.at[side, row_from, :], ms_got.at[side, row_to, :]
         else:
-            source, target = ms_own.at[:, row_from, :], ms_vert.at[0 if down > 0 else 1]
+            source, target = ms_tall.at[0 if down > 0 else 1], ms_vert.at[0 if down > 0 else 1]
         steps.append((down, right))
         copies.append(
             pltpu.make_async_remote_copy(
@@ -252,7 +259,26 @@
     start_all(steps, copies)
     row_matrix = band(row_tap_here[...], row_frac_here[...], 2 * HALO + rows, 0)
     col_matrix = band(col_tap_here[...], col_frac_here[...], 2 * LANES + cols, LANES - HALO)
-    ms_row_matrix = band(ms_row_tap_here[...], ms_row_frac_here[...], 32 + ms_rows, 16 - MHALO)
+    ms_row_taps = ms_row_tap_here[...]
+    ms_row_fracs = ms_row_frac_here[...]
+    ms_row_matrix = band(ms_row_taps, ms_row_fracs, 32 + ms_rows, 16 - MHALO)
+    line = lax.broadcasted_iota(jnp.int32, (32 + ms_rows, rows), 0)
+    below = 16 + ms_rows
+    away = -LANES
+    first_of_pair = jnp.where(
+        line < MHALO, line, jnp.where((line < 16) | (line >= below + MHALO), away, line - MHALO)
+    )
+    second_of_pair = jnp.where(
+        line < MHALO,
+        away,
+        jnp.where(
+            line < below, line - MHALO, jnp.where(line < below + MHALO, away, line - 2 * MHALO)
+        ),
+    )
+    ms_pair_matrices = tuple(
+        band_at(position, ms_row_taps, ms_row_fracs)
+        for position in (first_of_pair, second_of_pair)
+    )
     ms_col_taps = ms_col_tap_here[...]
     ms_col_fracs = ms_col_frac_here[...]
     ms_own_matrix = band(ms_col_taps, ms_col_fracs, ms_cols, -MHALO)
@@ -291,18 +317,37 @@
         clear(north_ok, ms_got.at[side, :16, :])
         clear(south_ok, ms_got.at[side, 16 + ms_rows :, :])
 
+    tall_steps, tall_copies = [], []
+
+    def send_rows(c):
+        for index, down in enumerate((1, -1)):
+            row_from, row_to = span(down, rows, EDGE)
+            tall_steps.append((down, 0))
+            tall_copies.append(
+                pltpu.make_async_remote_copy(
+                    src_ref=wide.at[c, slice(row_from.start + EDGE, row_from.stop + EDGE), :cols],
+                    dst_ref=wide.at[c, row_to, :cols],
+                    send_sem=send_tall.at[2 * c + index],
+                    recv_sem=recv_tall.at[2 * c + index],
+                    device_id=device(down, 0),
+                    device_id_type=MESH,
+                )
+            )
+        start_all(tall_steps[-2:], tall_copies[-2:])
+
     segment = dot_t(row_matrix, pan_patch[...]).astype(jnp.bfloat16)
     wide[0, EDGE : EDGE + rows, :cols] = dot(segment, col_matrix).astype(jnp.bfloat16)
     lane = lax.broadcasted_iota(jnp.int32, (rows, LANES), 1)
     halo_segment = dot_t(ms_row_matrix, ms_got[0]) + dot_t(ms_row_matrix, ms_got[1])
     halo_band = lax.rem(lane, ms_slot) // MHALO
     for b in range(bands):
-        block = jnp.concatenate([ms_vert[0, b], ms_own[b], ms_vert[1, b]], axis=0)
-        segment = dot_t(ms_row_matrix, block).astype(jnp.bfloat16)
+        block = jnp.concatenate([ms_vert[0, b // 2], ms_own[b], ms_vert[1, b // 2]], axis=0)
+        segment = dot_t(ms_pair_matrices[b % 2], block).astype(jnp.bfloat16)
         beside = jnp.where(halo_band == b, halo_segment, 0.0).astype(jnp.bfloat16)
         wide[b + 1, EDGE : EDGE + rows, :cols] = (
             dot(segment, ms_own_matrix) + dot(beside, ms_halo_matrix)
         ).astype(jnp.bfloat16)
+        send_rows(b)
 
     lane = lax.broadcasted_iota(jnp.int32, (LANES, 2 * LANES), 0)
     slot = lax.broadcasted_iota(jnp.int32, (LANES, 2 * LANES), 1)
@@ -318,13 +363,12 @@
     pack_east[...] = east_sum.astype(jnp.bfloat16)
     pack_west[...] = west_sum.astype(jnp.bfloat16)
 
+    send_rows(bands)
+    side_steps = tuple(step for step in STEPS if step[1])
     copies = []
-    for index, (down, right) in enumerate(STEPS):
+    for index, (down, right) in enumerate(side_steps):
         row_from, row_to = span(down, rows, EDGE)
-        if right == 0:
-            source = wide.at[:, slice(row_from.start + EDGE, row_from.stop + EDGE), :cols]
-            target = wide.at[:, row_to, :cols]
-        elif right > 0:
+        if right > 0:
             source, target = pack_east.at[row_from, :], got_west.at[row_to, :]
         else:
             source, target = pack_west.at[row_from, :], got_east.at[row_to, :]
@@ -338,8 +382,8 @@
                 device_id_type=MESH,
             )
         )
-    start_all(STEPS, copies)
-    wait_all(STEPS, copies)
+    start_all(side_steps, copies)
+    wait_all(tuple(tall_steps) + side_steps, tall_copies + copies)
 
     clear(north_ok, wide.at[:, :EDGE, :cols])
     clear(south_ok, wide.at[:, EDGE + rows :, :cols])
@@ -481,7 +525,8 @@
         + [pltpu.VMEM(table.shape, table.dtype) for table in tables]
         + [
             pltpu.VMEM((rows + 2 * HALO, cols + 2 * LANES), bf16),
-            pltpu.VMEM((2, bands, 16, ms_cols), bf16),
+            pltpu.VMEM((2, bands // 2, 16, ms_cols), bf16),
+            pltpu.VMEM((2, bands // 2, 16, ms_cols), bf16),
             pltpu.VMEM((2, rows * HALO // LANES, LANES), bf16),
             pltpu.VMEM((2, rows * HALO // LANES, LANES), bf16),
             pltpu.VMEM((2, ms_rows, LANES), bf16),
@@ -493,7 +538,8 @@
             dma,
             dma((len(tables) + 1,)),
         ]
-        + [dma((len(STEPS),))] * 6,
+        + [dma((len(STEPS),))] * 6
+        + [dma((2 * channels,))] * 2,
         compiler_params=pltpu.CompilerParams(collective_id=0, has_side_effects=True),
     )(pan_source.reshape(rows, cols), ms_source.reshape(bands, ms_rows, ms_cols), *tables)
     fit_rows = rows + EDGE

time: 48.6 us -> 47 us (0.967)
  Pallas kernels: 48.5 us -> 46.9 us
    pallas_call x1, Pallas kernels: 32.1 us -> 30.5 us  [local(): pl.pallas_call(functools.partial(resample_kernel, sec_count, tile_count),...]
where the time goes in v3:
time: 47 us; the launch traced here: 46.9 us
  Pallas kernels  46.9 us (100%)
    pallas_call x1, Pallas kernels, local(): pl.pallas_call(functools.partial(resample_kernel, sec_count, tile_count),...  30.5 us
    pallas_call x1, Pallas kernels, local(): pl.pallas_call(functools.partial(filter_kernel, sec_count, tile_count), g...  16.3 us

profile of v3, /device:TPU:5, one launch (start us, length us, event | category | flops | bytes accessed | tf_op | source)
XLA Modules:
  0.0 46.9 jit_solution(14898616330621690017)
XLA Ops:
  0.0 30.5 %shard_map.100.guide.bandref = bf16[9,288,512]{2,1,0:T(8,128)(2,1)} custom-call(bf16[256,384]{1,0:T(8,128)(2,1)} %bitcast.5, bf16[8,64,96]{2,1,0:T(8,128)(2,1)} %bitcast.6, s32[1,256]{1,0:T(1,128)} %row_tap.1, f32[1,256]{1,0:T(1,128)} %row_frac.1, s32[1,384]{1,0:T(1,128)} %col_tap.1, f32[1,384]{1,0:T(1,128)} %col_frac.1, s32[1,256]{1,0:T(1,128)} %ms_row_tap.1, ...), custom_call_target="tpu_custom_call" | custom-call | tf_op jit(solution)/shard_map/pallas_call | solution.py:519
  30.5 16.3 %shard_map.101 = bf16[8,256,384]{2,1,0:T(8,128)(2,1)} custom-call(bf16[9,288,512]{2,1,0:T(8,128)(2,1)} %shard_map.100.guide.bandref, bf16[9,288,512]{2,1,0:T(8,128)(2,1)} %shard_map.100.guide.bandref), custom_call_target="tpu_custom_call" | custom-call | tf_op jit(solution)/shard_map/pallas_call | solution.py:546

commit v4 on v3

--- a/solution.py
+++ b/solution.py
@@ -405,12 +405,17 @@
         ).astype(jnp.bfloat16)
 
 
-def sum_down(values, kept):
-    count = values.shape[0]
-    total = values
-    for shift in (1, 2, 4):
-        total = total + pltpu.roll(total, count - shift, 0)
-    return total[:kept] + total[8 : kept + 8] + values[16 : kept + 16]
+def sum_down(lines, pairs, fours, kept):
+    count = kept + EDGE
+    pairs[:count] = lines[:count] + lines[1 : count + 1]
+    fours[:count] = pairs[:count] + pairs[2 : count + 2]
+    eights = fours[: kept + 8] + fours[4 : kept + 12]
+    return eights[:kept] + eights[8:] + lines[EDGE:count]
+
+
+def store_chunks(target, values):
+    for t in range(values.shape[1] // LANES):
+        target[t, : values.shape[0]] = values[:, t * LANES : (t + 1) * LANES]
 
 
 def inverse_cover(first, shape, axis, extent, kept):
@@ -439,6 +444,8 @@
     sums_b,
     fit_a,
     fit_b,
+    pairs,
+    fours,
 ):
     wide_rows, width = guide.shape[1:]
     rows, cols = out.shape[1:]
@@ -474,36 +481,35 @@
             col0, (rows, cols), 1, map_cols, cols
         )
         own = guide[0].astype(jnp.float32)
-        sums_a[...] = dot(guide[0], box_a[...])
-        sums_b[...] = box_across(own * own, box_a[...])
+        store_chunks(sums_a, dot(guide[0], box_a[...]))
+        store_chunks(sums_b, box_across(own * own, box_a[...]))
         for t in range(chunks):
             lanes = slice(t * LANES, (t + 1) * LANES)
             scale = inverse[:, lanes]
-            mean = sum_down(sums_a[:, lanes], fit_rows) * scale
-            square = sum_down(sums_b[:, lanes], fit_rows) * scale
+            mean = sum_down(sums_a.at[t], pairs.at[2 * t + 0], fours.at[2 * t + 0], fit_rows) * scale
+            square = sum_down(sums_b.at[t], pairs.at[2 * t + 1], fours.at[2 * t + 1], fit_rows) * scale
             mean_guide[:, lanes] = mean
             inverse_var[:, lanes] = 1.0 / (square - mean * mean + EPSILON)
 
-    sums_a[...] = dot(bandref[0], box_a[...])
-    sums_b[...] = box_across(
-        guide[0].astype(jnp.float32) * bandref[0].astype(jnp.float32), box_a[...]
-    )
+    store_chunks(sums_a, dot(bandref[0], box_a[...]))
+    product = guide[0].astype(jnp.float32) * bandref[0].astype(jnp.float32)
+    store_chunks(sums_b, box_across(product, box_a[...]))
     for t in range(chunks):
         lanes = slice(t * LANES, (t + 1) * LANES)
         scale = inverse[:, lanes]
         mean = mean_guide[:, lanes]
-        mean_band = sum_down(sums_a[:, lanes], fit_rows) * scale
-        cross = sum_down(sums_b[:, lanes], fit_rows) * scale
+        mean_band = sum_down(sums_a.at[t], pairs.at[2 * t + 0], fours.at[2 * t + 0], fit_rows) * scale
+        cross = sum_down(sums_b.at[t], pairs.at[2 * t + 1], fours.at[2 * t + 1], fit_rows) * scale
         gain = (cross - mean * mean_band) * inverse_var[:, lanes]
         fit_a[:, lanes] = gain.astype(jnp.bfloat16)
         fit_b[:, lanes] = (mean_band - gain * mean).astype(jnp.bfloat16)
-    sums_a[:fit_rows, :cols] = dot(fit_a[...], box_b[...])
-    sums_b[:fit_rows, :cols] = dot(fit_b[...], box_b[...])
+    store_chunks(sums_a, dot(fit_a[...], box_b[...]))
+    store_chunks(sums_b, dot(fit_b[...], box_b[...]))
     for t in range(cols // LANES):
         lanes = slice(t * LANES, (t + 1) * LANES)
         own = guide[0, EDGE : EDGE + rows, lanes].astype(jnp.float32)
-        gain = sum_down(sums_a[:fit_rows, lanes], rows)
-        offset = sum_down(sums_b[:fit_rows, lanes], rows)
+        gain = sum_down(sums_a.at[t], pairs.at[2 * t + 0], fours.at[2 * t + 0], rows)
+        offset = sum_down(sums_b.at[t], pairs.at[2 * t + 1], fours.at[2 * t + 1], rows)
         out[0, :, lanes] = ((gain * own + offset) * inverse_out[:, lanes]).astype(jnp.bfloat16)
 
 
@@ -559,10 +565,12 @@
             pltpu.VMEM((rows, cols), f32),
             pltpu.VMEM((fit_rows, width), f32),
             pltpu.VMEM((fit_rows, width), f32),
-            pltpu.VMEM((wide_rows, width), f32),
-            pltpu.VMEM((wide_rows, width), f32),
+            pltpu.VMEM((width // LANES, wide_rows + EDGE, LANES), f32),
+            pltpu.VMEM((width // LANES, wide_rows + EDGE, LANES), f32),
             pltpu.VMEM((fit_rows, width), bf16),
             pltpu.VMEM((fit_rows, width), bf16),
+            pltpu.VMEM((2 * width // LANES, wide_rows + EDGE, LANES), f32),
+            pltpu.VMEM((2 * width // LANES, wide_rows + EDGE, LANES), f32),
         ],
     )(wide, wide)
     return sharpened[:, None]

time: 47 us -> 46.1 us (0.981)
  Pallas kernels: 46.9 us -> 45.9 us
    pallas_call x1, Pallas kernels: 16.3 us -> 15.4 us  [local(): pl.pallas_call(functools.partial(filter_kernel, sec_count, tile_count), g...]
where the time goes in v4:
time: 46.1 us; the launch traced here: 46 us
  Pallas kernels  45.9 us (100%)
    pallas_call x1, Pallas kernels, local(): pl.pallas_call(functools.partial(resample_kernel, sec_count, tile_count),...  30.5 us
    pallas_call x1, Pallas kernels, local(): pl.pallas_call(functools.partial(filter_kernel, sec_count, tile_count), g...  15.4 us

profile of v4, /device:TPU:5, one launch (start us, length us, event | category | flops | bytes accessed | tf_op | source)
XLA Modules:
  0.0 46.0 jit_solution(5052777155771245069)
XLA Ops:
  0.0 30.5 %shard_map.100.guide.bandref = bf16[9,288,512]{2,1,0:T(8,128)(2,1)} custom-call(bf16[256,384]{1,0:T(8,128)(2,1)} %bitcast.5, bf16[8,64,96]{2,1,0:T(8,128)(2,1)} %bitcast.6, s32[1,256]{1,0:T(1,128)} %row_tap.1, f32[1,256]{1,0:T(1,128)} %row_frac.1, s32[1,384]{1,0:T(1,128)} %col_tap.1, f32[1,384]{1,0:T(1,128)} %col_frac.1, s32[1,256]{1,0:T(1,128)} %ms_row_tap.1, ...), custom_call_target="tpu_custom_call" | custom-call | tf_op jit(solution)/shard_map/pallas_call | solution.py:525
  30.5 15.4 %shard_map.101 = bf16[8,256,384]{2,1,0:T(8,128)(2,1)} custom-call(bf16[9,288,512]{2,1,0:T(8,128)(2,1)} %shard_map.100.guide.bandref, bf16[9,288,512]{2,1,0:T(8,128)(2,1)} %shard_map.100.guide.bandref), custom_call_target="tpu_custom_call" | custom-call | tf_op jit(solution)/shard_map/pallas_call | solution.py:552
